TPU v7x, 256 devices: a whole 4x4x8 slice. The times are simulated.
256 devices in a mesh: row: 8 (over y_hi, x), col: 32 (over y_lo, z, core).
Axes of the slice: x: 4, y: 4 (y_hi: 2, y_lo: 2; y = y_hi * 2 + y_lo), z: 8, core: 2. Of those that a mesh axis runs over, the one named last changes fastest.
Arguments:
- sectors: int32 [96], replicated, may hold values from 0 to 7
- environment: bfloat16 [24576, 24576], P('col', 'row'), may hold values from -0.109375 to 0.109375
- wavefunction: bfloat16 [24576, 2048], P('row', 'col'), may hold values from -6 to 6
Outputs:
- applied: bfloat16 [24576, 2048], P('col', 'row')
All inputs are finite; a program needn't handle non-finite values.
Results may differ from a plain program's by a relative error of at most 0.013.
Values may be sent and summed in bfloat16 or wider, within the bound.
A program may use at most 64 MiB of HBM per device.

v0:
```python
import jax
import jax.numpy as jnp
from jax import lax
from jax.sharding import PartitionSpec as P

BLOCK = 256


def body(sectors, environment, wavefunction):
    row_tile, col_tile = environment.shape
    row_blocks = row_tile // BLOCK
    col_blocks = col_tile // BLOCK
    row_sector = lax.dynamic_slice_in_dim(sectors, lax.axis_index("col") * row_blocks, row_blocks)
    col_sector = lax.dynamic_slice_in_dim(sectors, lax.axis_index("row") * col_blocks, col_blocks)
    allowed = row_sector[:, None] == col_sector[None, :]
    allowed = jnp.repeat(jnp.repeat(allowed, BLOCK, axis=0), BLOCK, axis=1)
    masked = jnp.where(allowed, environment, jnp.zeros_like(environment))
    gathered = lax.all_gather(wavefunction, "col", axis=1, tiled=True)
    reduced = lax.psum_scatter(
        jnp.dot(masked, gathered, preferred_element_type=jnp.float32).astype(jnp.bfloat16),
        "row",
        scatter_dimension=0,
        tiled=True,
    )
    result = lax.all_to_all(reduced, "row", split_axis=1, concat_axis=0, tiled=True)
    return result


def solution(mesh):
    placed = (P(), P("col", "row"), P("row", "col"))
    return jax.shard_map(
        body, mesh=mesh, in_specs=placed, out_specs=P("col", "row"), check_vma=False
    )
```

profile of v0, /device:TPU:12, one launch (start us, length us, event | category | flops | bytes accessed | tf_op | source)
XLA Modules:
  0.0 213.3 jit_solution(13569756071219701968)
XLA Ops:
  6.5 0.0 all-gather.2.cloned.1.call-start
  6.5 0.7 all-gather.2.cloned.1.call-update
  7.3 0.0 reduce-scatter.2.cloned.1.call-start
  7.3 0.7 dynamic_slice.7
  8.0 0.7 dynamic_slice.6
  8.8 0.1 broadcast_compare_fusion
  8.8 0.1 broadcast_bitcast_fusion
  9.0 6.6 %copy.7 = bf16[768,3072]{0,1:T(8,128)(2,1)} copy(bf16[768,3072]{1,0:T(8,128)(2,1)} %param.4) | data formatting | bytes 9437184 | tf_op args[1]
  15.6 4.7 %bitcast_select_fusion = bf16[768,3072]{0,1:T(8,128)(2,1)} fusion(bf16[768,3072]{0,1:T(8,128)(2,1)} %copy.7, pred[768,12]{0,1:T(8,128)(4,1)S(1)} %bitcast.21), kind=kLoop, calls=%fused_computation | loop fusion | flops 2359296 | bytes 9446400 | tf_op jit(solution)/shard_map/jit(_where)/select_n | solution.py:17
  20.4 71.4 %all-gather.2.cloned.1.call-done = bf16[3072,2048]{0,1:T(8,128)(2,1)} async-done(((bf16[3072,64]{0,1:T(8,128)(2,1)}), bf16[3072,2048]{0,1:T(8,128)(2,1)}) %all-gather.2.cloned.1.call-update) | async-done | bytes 12582928 | tf_op jit(solution)/shard_map/all_gather | solution.py:18
  91.8 15.5 %convolution_convert_fusion = bf16[768,2048]{1,0:T(8,128)(2,1)} fusion(bf16[768,3072]{0,1:T(8,128)(2,1)} %bitcast_select_fusion, bf16[3072,2048]{0,1:T(8,128)(2,1)} %all-gather.2.cloned.1.call-done), kind=kOutput, calls=%fused_computation.1 | convolution fusion | flops 9665249280 | bytes 20447232 | tf_op jit(solution)/shard_map/dot_general | solution.py:20
  107.3 0.0 reduce-scatter.2.cloned.1.call-update
  107.3 83.9 %reduce-scatter.2.cloned.1.call-done = bf16[96,2048]{1,0:T(8,128)(2,1)} async-done(((bf16[768,2048]{1,0:T(8,128)(2,1)}), bf16[96,2048]{1,0:T(8,128)(2,1)}) %reduce-scatter.2.cloned.1.call-update) | async-done | bytes 393232 | tf_op jit(solution)/shard_map/reduce_scatter | solution.py:19
  191.2 1.0 copy.12
  192.2 13.4 %all_to_all.19 = bf16[96,8,256]{2,0,1:T(8,128)(2,1)S(1)} all-to-all(bf16[96,8,256]{2,0,1:T(8,128)(2,1)S(1)} %bitcast.17), channel_id=1, replica_groups=mesh['row'=8,'col'=32] {'row'}, dimensions={1} | all-to-all | bytes 786432 | tf_op jit(solution)/shard_map/all_to_all | solution.py:25
  205.7 0.7 copy.14
  (2 shorter events, 0.0 us)
Async XLA Ops:
  6.5 85.2 %all-gather.2.cloned.1.call-start = ((), (), s32[]{:S(2)}) async-start(), calls=%async_computation.2 | async-start | bytes 12976128 | tf_op jit(solution)/shard_map/all_gather | solution.py:18
  7.3 184.0 %reduce-scatter.2.cloned.1.call-start = ((), (), s32[]{:S(2)}) async-start(), calls=%async_computation.3 | async-start | bytes 3538944 | tf_op jit(solution)/shard_map/reduce_scatter | solution.py:19
Sparse Core Ops, SparseCore 0:
  9.2 82.5 all-gather.1
  107.5 83.7 reduce-scatter.1
where the time goes:
time: 216 us; the launch traced here: 213 us
  waiting for transfers between devices  156 us (72%)
  matrix products  15.5 us (7%)
  blocking collectives  13.4 us (6%)
  between operations  13.4 us (6%)
  local copies, waits for them, and re-layouts  9.97 us (5%)
  other arithmetic  4.82 us (2%)
    reduce_scatter x1, waiting for transfers between devices, body(): lax.psum_scatter(jnp.dot(masked, gathered, preferred_element_type=jnp.flo...  83.9 us
    all_gather x1, waiting for transfers between devices, body(): gathered = lax.all_gather(wavefunction, 'col', axis=1, tiled=True)  71.4 us
    dot_general x1, matrix products, body(): jnp.dot(masked, gathered, preferred_element_type=jnp.float32)  15.5 us
    all_to_all x1, blocking collectives, body(): lax.all_to_all(reduced, 'row', split_axis=1, concat_axis=0, tiled=True)  13.4 us
    unnamed x5, local copies, waits for them, and re-layouts  7.49 us
    select_n x1, other arithmetic, body(): masked = jnp.where(allowed, environment, jnp.zeros_like(environment))  4.75 us
  transfers between devices with their start and end apart: 2, of which 2 were waited for; matrix products, arithmetic and copies ran while one was open for 6% of the time, Pallas kernels for 0%

commit v1 on v0

v1 whole, which is shorter than its diff:
```python
import jax
import jax.numpy as jnp
from jax import lax
from jax.experimental import pallas as pl
from jax.experimental.pallas import tpu as pltpu
from jax.sharding import PartitionSpec as P

MESH = pl.DeviceIdType.MESH
BLOCK = 256
ITEM = 64
ROWS = 768
DEPTH = 3072
HALF = DEPTH // 2
TILE = 256
CHUNK = ROWS // 4

FULL = (0, ITEM, 0, DEPTH)
H0 = (0, ITEM, 0, HALF)
H1 = (0, ITEM, HALF, HALF)
H1LO = (0, ITEM // 2, HALF, HALF)
H1HI = (ITEM // 2, ITEM // 2, HALF, HALF)

ZP = [(0, 0, FULL), (1, 0, H1), (0, -1, FULL), (1, -1, H1), (0, -2, FULL), (1, -2, H1), (0, -3, H0), (1, -3, H1LO)]
ZM = [(0, 0, FULL), (1, 0, H1), (0, 1, FULL), (1, 1, H1), (0, 2, FULL), (1, 2, H1), (0, 3, H1), (1, 3, H1HI)]
YY = [(0, 0, H1), (0, 0, H0)] + [(0, s * d, H0) for d in (1, 2, 3) for s in (-1, 1)] + [(0, 4, H0)]
CC = [(0, 0, FULL), (1, 0, H1), (1, 0, H0)]
for _d in (1, 2, 3):
    CC += [(0, -_d, FULL), (0, _d, FULL), (1, -_d, H1), (1, _d, H1), (1, -_d, H0), (1, _d, H0)]
CC += [(0, 4, H0), (0, 4, H1), (1, 4, H1LO), (1, 4, H1HI), (1, 4, H0)]
LINKS = {"zp": ZP, "zm": ZM, "y": YY, "c": CC}


def kernel(sec_ref, env_ref, wave_ref, out_ref, a, g, cb, rb, red, fin,
           s_zp, r_zp, s_zm, r_zm, s_y, r_y, s_c, r_c, s_x, r_x, s_f, r_f, local):
    row, col = lax.axis_index("row"), lax.axis_index("col")
    yh, x = row // 4, row % 4
    y, z, c = col // 16, (col // 2) % 8, col % 2

    def device(dyh=0, dx=0, dy=0, dz=0, dc=0):
        return (
            (yh + dyh) % 2 * 4 + (x + dx) % 4,
            (y + dy) % 2 * 16 + (z + dz + 8) % 8 * 2 + (c + dc) % 2,
        )

    load_a = pltpu.make_async_copy(env_ref, a, local.at[0])
    load_a.start()
    own = pl.ds(pl.multiple_of(col * ITEM, ITEM), ITEM)
    load_b = pltpu.make_async_copy(wave_ref, g.at[own, :], local.at[1])
    load_b.start()

    barrier = pltpu.get_barrier_semaphore()
    greet = [device(dz=1), device(dz=-1), device(dy=1), device(dc=1)]
    greet += [device(dyh=h, dx=d) for h in (0, 1) for d in range(4) if (h, d) != (0, 0)]
    for peer in greet:
        pl.semaphore_signal(barrier, inc=1, device_id=peer, device_id_type=MESH)
    load_b.wait()
    pl.semaphore_wait(barrier, len(greet))

    sems = {"zp": (s_zp, r_zp), "zm": (s_zm, r_zm), "y": (s_y, r_y), "c": (s_c, r_c)}
    peers = {"zp": device(dz=1), "zm": device(dz=-1), "y": device(dy=1), "c": device(dc=1)}
    moves = {"zp": (0, -1, 0), "zm": (0, 1, 0), "y": (1, 0, 0), "c": (0, 0, 1)}

    def piece(line, d, part, parity):
        r0, nr, k0, nk = part
        j = (y + line) % 2 * 16 + (z + d + 8) % 8 * 2 + (c + parity) % 2
        return g.at[pl.ds(pl.multiple_of(j * ITEM + r0, 32), nr), pl.ds(k0, nk)]

    started = []

    def copy(link, ref, i):
        return pltpu.make_async_remote_copy(
            src_ref=ref, dst_ref=ref, send_sem=sems[link][0].at[i], recv_sem=sems[link][1].at[i],
            device_id=peers[link], device_id_type=MESH,
        )

    def send(link, line, d, part):
        i = LINKS[link].index((line, d, part))
        cp = copy(link, piece(line, d, part, 0), i)
        cp.start()
        started.append(cp)

    def recv(link, line, d, part):
        dl, dz, dc = moves[link]
        sd = d - dz
        sd = {-4: 4, 5: -3, -5: 3}.get(sd, sd)
        i = LINKS[link].index(((line + dl) % 2, sd, part))
        copy(link, piece(line, d, part, dc), i).wait_recv()

    def hop(link, line, d, part, onward):
        recv(link, line, d, part)
        for to, sub in onward:
            send(to, line, d, sub)

    def core(line, d, part):
        recv("c", line, d, part)

    odd = z % 2
    q0 = z // 2
    turn = 1 - 2 * odd
    quads = [q0, (q0 - turn + 4) % 4, (q0 + turn + 4) % 4, (q0 + 2) % 4]

    def compute(line, phase):
        t = phase * 2 + line
        base = (y + line) % 2 * 1024 + quads[phase] * TILE
        block = g[pl.ds(pl.multiple_of(base, TILE), TILE), :]

        cb[t] = lax.dot_general(
            a[...], block, (((1,), (1,)), ((), ())), preferred_element_type=jnp.float32
        ).astype(jnp.bfloat16)
        for d in (1, 2, 3):
            to = (x + d) % 4
            cp = pltpu.make_async_remote_copy(
                src_ref=cb.at[t, pl.ds(pl.multiple_of(to * CHUNK, CHUNK), CHUNK), :],
                dst_ref=rb.at[t, x], send_sem=s_x.at[t, d], recv_sem=r_x.at[t, x],
                device_id=device(dx=d), device_id_type=MESH,
            )
            cp.start()
            started.append(cp)

    def reduce(line, phase):
        t = phase * 2 + line
        mine = pl.ds(pl.multiple_of(x * CHUNK, CHUNK), CHUNK)
        total = cb[t, mine, :].astype(jnp.float32)
        for d in (1, 2, 3):
            src = (x + d) % 4
            pltpu.make_async_remote_copy(
                src_ref=cb.at[t, mine, :], dst_ref=rb.at[t, src], send_sem=s_x.at[t, d],
                recv_sem=r_x.at[t, src], device_id=device(dx=d), device_id_type=MESH,
            ).wait_recv()
            total += rb[t, src].astype(jnp.float32)
        to = (y + line) % 2 * 4 + quads[phase]

        @pl.when(to == row)
        def _():
            fin[row] = total.astype(jnp.bfloat16)

        @pl.when(to != row)
        def _():
            red[t] = total.astype(jnp.bfloat16)
            final(t, to).start()

    def final(t, to):
        return pltpu.make_async_remote_copy(
            src_ref=red.at[t], dst_ref=fin.at[row], send_sem=s_f.at[t], recv_sem=r_f.at[row],
            device_id=(to, col), device_id_type=MESH,
        )

    send("zp", 0, 0, FULL)
    send("zm", 0, 0, FULL)
    send("y", 0, 0, H1)
    send("y", 0, 0, H0)
    send("c", 0, 0, FULL)

    load_a.wait()
    for i in range(ROWS // BLOCK):
        for k in range(DEPTH // BLOCK):
            keep = sec_ref[col * (ROWS // BLOCK) + i] == sec_ref[row * (DEPTH // BLOCK) + k]
            at = (pl.ds(i * BLOCK, BLOCK), pl.ds(k * BLOCK, BLOCK))
            a[at] = jnp.where(keep, a[at], jnp.zeros((BLOCK, BLOCK), a.dtype))

    hop("y", 1, 0, H1, [("zp", H1), ("zm", H1), ("c", H1)])
    hop("zp", 0, -1, FULL, [("zp", FULL), ("y", H0), ("c", FULL)])
    hop("zm", 0, 1, FULL, [("zm", FULL), ("y", H0), ("c", FULL)])
    hop("y", 1, 0, H0, [("c", H0)])
    core(0, 0, FULL), core(0, -1, FULL), core(0, 1, FULL)
    compute(0, 0)
    hop("zp", 1, -1, H1, [("zp", H1), ("c", H1)])
    hop("zm", 1, 1, H1, [("zm", H1), ("c", H1)])
    hop("y", 1, -1, H0, [("c", H0)])
    hop("y", 1, 1, H0, [("c", H0)])
    reduce(0, 0)
    hop("zp", 0, -2, FULL, [("zp", FULL), ("y", H0), ("c", FULL)])
    hop("zm", 0, 2, FULL, [("zm", FULL), ("y", H0), ("c", FULL)])
    core(1, 0, H1), core(1, 0, H0), core(1, -1, H1), core(1, 1, H1), core(1, -1, H0), core(1, 1, H0)
    compute(1, 0)
    hop("zp", 1, -2, H1, [("zp", H1), ("c", H1)])
    hop("zm", 1, 2, H1, [("zm", H1), ("c", H1)])
    core(0, -2, FULL), core(0, 2, FULL)
    compute(0, 1)
    reduce(1, 0)
    hop("y", 1, -2, H0, [("c", H0)])
    hop("y", 1, 2, H0, [("c", H0)])
    hop("zp", 0, -3, FULL, [("zp", H0), ("y", H0), ("c", FULL)])
    hop("zm", 0, 3, FULL, [("zm", H1), ("y", H0), ("c", FULL)])
    core(1, -2, H1), core(1, 2, H1), core(1, -2, H0), core(1, 2, H0)
    compute(1, 1)
    reduce(0, 1)
    hop("zp", 1, -3, H1, [("zp", H1LO), ("c", H1)])
    hop("zm", 1, 3, H1, [("zm", H1HI), ("c", H1)])
    core(0, -3, FULL), core(0, 3, FULL)
    compute(0, 2)
    reduce(1, 1)
    hop("y", 1, -3, H0, [("c", H0)])
    hop("zp", 0, 4, H0, [("y", H0), ("c", H0)])
    hop("zm", 0, 4, H1, [("c", H1)])
    hop("y", 1, 3, H0, [("c", H0)])
    core(1, -3, H1), core(1, 3, H1), core(1, -3, H0), core(1, 3, H0)
    compute(1, 2)
    hop("zp", 1, 4, H1LO, [("c", H1LO)])
    hop("zm", 1, 4, H1HI, [("c", H1HI)])
    core(0, 4, H0), core(0, 4, H1)
    compute(0, 3)
    reduce(0, 2)
    hop("y", 1, 4, H0, [("c", H0)])
    core(1, 4, H1LO), core(1, 4, H1HI), core(1, 4, H0)
    compute(1, 3)
    reduce(1, 2)
    reduce(0, 3)
    reduce(1, 3)

    for h, d in [(h, d) for d in range(4) for h in (0, 1) if (h, d) != (0, 0)]:
        src = (yh + h) % 2 * 4 + (x + d) % 4
        pltpu.make_async_remote_copy(
            src_ref=red.at[0], dst_ref=fin.at[src], send_sem=s_f.at[0], recv_sem=r_f.at[src],
            device_id=device(dyh=h, dx=d), device_id_type=MESH,
        ).wait_recv()
    for part in range(4):
        out_ref[part * CHUNK : (part + 1) * CHUNK, :] = (
            fin[part].astype(jnp.float32) + fin[4 + part].astype(jnp.float32)
        ).astype(out_ref.dtype)

    for cp in started:
        cp.wait_send()
    for line in (0, 1):
        for phase in range(4):
            to = (y + line) % 2 * 4 + quads[phase]

            @pl.when(to != row)
            def _():
                final(phase * 2 + line, to).wait_send()


def body(sectors, environment, wavefunction):
    dma = pltpu.SemaphoreType.DMA
    pairs = []
    for link in ("zp", "zm", "y", "c"):
        pairs += [dma((len(LINKS[link]),)), dma((len(LINKS[link]),))]
    return pl.pallas_call(
        kernel,
        out_shape=jax.ShapeDtypeStruct((ROWS, TILE), jnp.bfloat16),
        in_specs=[
            pl.BlockSpec(memory_space=pltpu.SMEM),
            pl.BlockSpec(memory_space=pl.ANY),
            pl.BlockSpec(memory_space=pl.ANY),
        ],
        out_specs=pl.BlockSpec(memory_space=pltpu.VMEM),
        scratch_shapes=[
            pltpu.VMEM((ROWS, DEPTH), jnp.bfloat16),
            pltpu.VMEM((32 * ITEM, DEPTH), jnp.bfloat16),
            pltpu.VMEM((8, ROWS, TILE), jnp.bfloat16),
            pltpu.VMEM((8, 4, CHUNK, TILE), jnp.bfloat16),
            pltpu.VMEM((8, CHUNK, TILE), jnp.bfloat16),
            pltpu.VMEM((8, CHUNK, TILE), jnp.bfloat16),
            *pairs,
            dma((8, 4)), dma((8, 4)), dma((8,)), dma((8,)), dma((2,)),
        ],
        compiler_params=pltpu.CompilerParams(
            collective_id=0, has_side_effects=True, vmem_limit_bytes=56 << 20
        ),
    )(sectors, environment, wavefunction.T)


def solution(mesh):
    placed = (P(), P("col", "row"), P("row", "col"))
    return jax.shard_map(
        body, mesh=mesh, in_specs=placed, out_specs=P("col", "row"), check_vma=False
    )
```

time: 216 us -> 96.3 us (0.45); the launches traced: 213 us -> 95.9 us
  waiting for transfers between devices: 156 us -> 0 us
  Pallas kernels: 0 us -> 94.2 us
  matrix products: 15.5 us -> 0 us
  blocking collectives: 13.4 us -> 0 us
  between operations: 13.4 us -> 0.01 us
  local copies, waits for them, and re-layouts: 9.97 us -> 1.77 us
  other arithmetic: 4.82 us -> 0 us
    pallas_call x0 -> x1, Pallas kernels: none -> 94.2 us  [body(): pl.pallas_call(kernel, out_shape=jax.ShapeDtypeStruct((ROWS, TILE), jnp.b...]
    reduce_scatter x1 -> x0, waiting for transfers between devices: 83.9 us -> none  [body(): lax.psum_scatter(jnp.dot(masked, gathered, preferred_element_type=jnp.flo...]
    all_gather x1 -> x0, waiting for transfers between devices: 71.4 us -> none  [body(): gathered = lax.all_gather(wavefunction, 'col', axis=1, tiled=True)]
    dot_general x1 -> x0, matrix products: 15.5 us -> none  [body(): jnp.dot(masked, gathered, preferred_element_type=jnp.float32)]
    all_to_all x1 -> x0, blocking collectives: 13.4 us -> none  [body(): lax.all_to_all(reduced, 'row', split_axis=1, concat_axis=0, tiled=True)]
    unnamed x5 -> x1, local copies, waits for them, and re-layouts: 7.49 us -> 1.77 us
    select_n x1 -> x0, other arithmetic: 4.75 us -> none  [body(): masked = jnp.where(allowed, environment, jnp.zeros_like(environment))]
  transfers between devices with their start and end apart: 2 -> 0, of which waited for: 2 -> 0; matrix products, arithmetic and copies ran while one was open for 6% -> 0% of each run, Pallas kernels for 0% -> 0%
where the time goes in v1:
time: 96.3 us; the launch traced here: 95.9 us
  Pallas kernels  94.2 us (98%)
  local copies, waits for them, and re-layouts  1.77 us (2%)
    pallas_call x1, Pallas kernels, body(): pl.pallas_call(kernel, out_shape=jax.ShapeDtypeStruct((ROWS, TILE), jnp.b...  94.2 us

profile of v1, /device:TPU:12, one launch (start us, length us, event | category | flops | bytes accessed | tf_op | source)
XLA Modules:
  0.0 95.9 jit_solution(18127109685549770734)
XLA Ops:
  0.0 94.2 %shard_map.37 = bf16[768,256]{1,0:T(8,128)(2,1)} custom-call(s32[96]{0:T(128)} %sec_ref.1, bf16[768,3072]{1,0:T(8,128)(2,1)} %env_ref.1, bf16[64,3072]{1,0:T(8,128)(2,1)} %bitcast.1), custom_call_target="tpu_custom_call" | custom-call | tf_op jit(solution)/shard_map/pallas_call | solution.py:238
  94.2 1.8 %copy.5 = bf16[768,256]{1,0:T(8,128)(2,1)} copy(bf16[768,256]{1,0:T(8,128)(2,1)} %shard_map.37) | data formatting | bytes 786432

commit v2 on v0

v2 whole, which is shorter than its diff:
```python
import jax
import jax.numpy as jnp
from jax import lax
from jax.experimental import pallas as pl
from jax.experimental.pallas import tpu as pltpu
from jax.sharding import PartitionSpec as P

MESH = pl.DeviceIdType.MESH
BLOCK = 256
ITEM = 64
PAIR = 2 * ITEM
ROWS = 768
DEPTH = 3072
HALF = DEPTH // 2
TILE = 256
CHUNK = ROWS // 4

H0 = (0, ITEM, 0, HALF)
H1 = (0, ITEM, HALF, HALF)
LO = (0, ITEM // 2, HALF, HALF)
HI = (ITEM // 2, ITEM // 2, HALF, HALF)

DIST = [0, -1, 1, -2, 2, -3, 3, 4]

ZP = [(0, -d, h) for d in range(3) for h in (H0, H1)] + [(1, -d, H1) for d in range(3)] + [(0, -3, H0), (1, -3, LO)]
ZM = [(0, d, h) for d in range(3) for h in (H0, H1)] + [(1, d, H1) for d in range(3)] + [(0, 3, H1), (1, 3, HI)]
YY = [(0, 0, H1)] + [(0, d, H0) for d in DIST]
CC = [(line, d, h) for line in (0, 1) for d in DIST for h in (H0, H1) if (line, d, h) != (1, 4, H1)]
CC += [(1, 4, LO), (1, 4, HI)]
LINKS = {"zp": ZP, "zm": ZM, "y": YY, "c": CC}

ORDER = [
    ("mm", 0, 0),
    ("zp", 0, -1, H0),
    ("zm", 0, 1, H0),
    ("y", 1, 0, H1),
    ("ra", 0, 0),
    ("zp", 0, -1, H1),
    ("zm", 0, 1, H1),
    ("y", 1, 0, H0),
    ("mm", 0, -1),
    ("mm", 0, 1),
    ("y", 1, -1, H0),
    ("zp", 0, -2, H0),
    ("zm", 0, 2, H0),
    ("mm", 1, 0),
    ("ra", 0, -1),
    ("zp", 1, -1, H1),
    ("zm", 1, 1, H1),
    ("y", 1, 1, H0),
    ("ra", 0, 1),
    ("mm", 1, -1),
    ("mm", 1, 1),
    ("zp", 0, -2, H1),
    ("zm", 0, 2, H1),
    ("y", 1, -2, H0),
    ("ra", 1, 0),
    ("mm", 0, -2),
    ("mm", 0, 2),
    ("zp", 0, -3, H0),
    ("zm", 0, 3, H0),
    ("y", 1, 2, H0),
    ("ra", 1, -1),
    ("ra", 1, 1),
    ("rb", 0),
    ("ra", 0, -2),
    ("zp", 1, -2, H1),
    ("zm", 1, 2, H1),
    ("mm", 1, -2),
    ("y", 1, -3, H0),
    ("ra", 0, 2),
    ("mm", 1, 2),
    ("zp", 0, -3, H1),
    ("zm", 0, 3, H1),
    ("mm", 0, -3),
    ("y", 1, 3, H0),
    ("ra", 1, -2),
    ("rb", -1),
    ("zm", 1, 3, H1),
    ("zp", 0, 4, H0),
    ("rb", 1),
    ("mm", 0, 3),
    ("ra", 1, 2),
    ("mm", 1, 3),
    ("rb", -2),
    ("ra", 0, -3),
    ("zp", 1, -3, H1),
    ("zm", 0, 4, H1),
    ("mm", 1, -3),
    ("y", 1, 4, H0),
    ("zm", 1, 4, HI),
    ("ra", 0, 3),
    ("rb", 2),
    ("mm", 0, 4),
    ("zp", 1, 4, LO),
    ("ra", 1, 3),
    ("mm", 1, 4),
    ("ra", 1, -3),
    ("rb", 3),
    ("ra", 0, 4),
    ("rb", -3),
    ("ra", 1, 4),
    ("rb", 4),
]


def onward(link, line, d, part):
    to = [("c", part)]
    if link == "y":
        return to + ([("zp", part), ("zm", part)] if part == H1 else [])
    if line == 0 and part == H0:
        to.append(("y", part))
    if abs(d) < 3:
        to.insert(0, (link, part))
    elif abs(d) == 3 and line == 1:
        to.insert(0, (link, LO if link == "zp" else HI))
    elif abs(d) == 3 and part == (H0 if link == "zp" else H1):
        to.insert(0, (link, part))
    return to


def kernel(sec_ref, env_ref, wave_ref, out_ref, a, g, cb, rb, keep, red, yr, done, fin,
           s_zp, r_zp, s_zm, r_zm, s_y, r_y, s_c, r_c, s_x, r_x, s_h, r_h, s_f, r_f, local):
    row, col = lax.axis_index("row"), lax.axis_index("col")
    yh, x = row // 4, row % 4
    y, z, c = col // 16, (col // 2) % 8, col % 2

    def device(dyh=0, dx=0, dy=0, dz=0, dc=0):
        return (
            (yh + dyh) % 2 * 4 + (x + dx) % 4,
            (y + dy) % 2 * 16 + (z + dz + 8) % 8 * 2 + (c + dc) % 2,
        )

    load_a = pltpu.make_async_copy(env_ref, a, local.at[0])
    own = pl.ds(pl.multiple_of(col * ITEM, ITEM), ITEM)
    load_b = pltpu.make_async_copy(wave_ref, g.at[own, :], local.at[1])
    load_b.start()
    load_a.start()

    barrier = pltpu.get_barrier_semaphore()
    greet = [device(dz=1), device(dz=-1), device(dy=1), device(dc=1), device(dyh=1)]
    greet += [device(dx=d) for d in (1, 2, 3)]
    for peer in greet:
        pl.semaphore_signal(barrier, inc=1, device_id=peer, device_id_type=MESH)
    load_b.wait()
    pl.semaphore_wait(barrier, len(greet))

    sems = {"zp": (s_zp, r_zp), "zm": (s_zm, r_zm), "y": (s_y, r_y), "c": (s_c, r_c)}
    peers = {"zp": device(dz=1), "zm": device(dz=-1), "y": device(dy=1), "c": device(dc=1)}
    moves = {"zp": (0, -1, 0), "zm": (0, 1, 0), "y": (1, 0, 0), "c": (0, 0, 1)}
    started = []

    def piece(line, d, part, parity):
        r0, nr, k0, nk = part
        j = (y + line) % 2 * 16 + (z + d + 8) % 8 * 2 + (c + parity) % 2
        return g.at[pl.ds(pl.multiple_of(j * ITEM + r0, 32), nr), pl.ds(k0, nk)]

    def copy(link, ref, i):
        return pltpu.make_async_remote_copy(
            src_ref=ref, dst_ref=ref, send_sem=sems[link][0].at[i], recv_sem=sems[link][1].at[i],
            device_id=peers[link], device_id_type=MESH,
        )

    def send(link, line, d, part):
        cp = copy(link, piece(line, d, part, 0), LINKS[link].index((line, d, part)))
        cp.start()
        started.append(cp)

    def recv(link, line, d, part):
        dl, dz, dc = moves[link]
        sd = d - dz
        sd = {-4: 4, 5: -3, -5: 3}.get(sd, sd)
        i = LINKS[link].index(((line + dl) % 2, sd, part))
        copy(link, piece(line, d, part, dc), i).wait_recv()

    def multiply(line, d):
        for part in (H0, LO, HI) if (line, d) == (1, 4) else (H0, H1):
            recv("c", line, d, part)
        t = DIST.index(d) * 2 + line
        base = (y + line) % 2 * (16 * ITEM) + (z + d + 8) % 8 * PAIR
        block = g[pl.ds(pl.multiple_of(base, PAIR), PAIR), :]
        cb[t] = lax.dot_general(
            a[...], block, (((1,), (1,)), ((), ())), preferred_element_type=jnp.float32
        ).astype(jnp.bfloat16)
        for dx in (2, 1, 3):
            cp = share(t, dx, (x + dx) % 4, x)
            cp.start()
            started.append(cp)

    def share(t, dx, chunk, slot):
        return pltpu.make_async_remote_copy(
            src_ref=cb.at[t, pl.ds(pl.multiple_of(chunk * CHUNK, CHUNK), CHUNK), :],
            dst_ref=rb.at[t, slot], send_sem=s_x.at[t, dx], recv_sem=r_x.at[t, slot],
            device_id=device(dx=dx), device_id_type=MESH,
        )

    def over_y(i):
        return pltpu.make_async_remote_copy(
            src_ref=red.at[i], dst_ref=yr.at[i], send_sem=s_h.at[i], recv_sem=r_h.at[i],
            device_id=device(dyh=1), device_id_type=MESH,
        )

    def add_x(line, d):
        i = DIST.index(d)
        t = i * 2 + line
        total = cb[t, pl.ds(pl.multiple_of(x * CHUNK, CHUNK), CHUNK), :].astype(jnp.float32)
        for dx in (1, 3, 2):
            src = (x + dx) % 4
            share(t, dx, x, src).wait_recv()
            total += rb[t, src].astype(jnp.float32)
        stays = (y + line) % 2 == yh

        @pl.when(stays)
        def _():
            keep[i] = total

        @pl.when(jnp.logical_not(stays))
        def _():
            red[i] = total.astype(jnp.bfloat16)
            over_y(i).start()

    def final(i, half, to):
        return pltpu.make_async_remote_copy(
            src_ref=done.at[i], dst_ref=fin.at[x, half], send_sem=s_f.at[i], recv_sem=r_f.at[x],
            device_id=(yh * 4 + to, col), device_id_type=MESH,
        )

    def add_y(d):
        i = DIST.index(d)
        over_y(i).wait_recv()
        total = (keep[i] + yr[i].astype(jnp.float32)).astype(jnp.bfloat16)
        at = (z + d + 8) % 8
        half, to = at % 2, at // 2

        @pl.when(to == x)
        def _():
            fin[x, half] = total

        @pl.when(to != x)
        def _():
            done[i] = total
            final(i, half, to).start()

    for part in (H0, H1):
        send("zp", 0, 0, part)
        send("zm", 0, 0, part)
    for part in (H1, H0):
        send("y", 0, 0, part)
    for part in (H0, H1):
        send("c", 0, 0, part)

    load_a.wait()
    for i in range(ROWS // BLOCK):
        for k in range(DEPTH // BLOCK):
            same = sec_ref[col * (ROWS // BLOCK) + i] == sec_ref[row * (DEPTH // BLOCK) + k]
            at = (pl.ds(i * BLOCK, BLOCK), pl.ds(k * BLOCK, BLOCK))
            a[at] = jnp.where(same, a[at], jnp.zeros((BLOCK, BLOCK), a.dtype))

    steps = {"mm": multiply, "ra": add_x, "rb": add_y}
    for name, *args in ORDER:
        if name in steps:
            steps[name](*args)
        else:
            recv(name, *args)
            line, d, _ = args
            for to, part in onward(name, *args):
                send(to, line, d, part)

    for dx in (1, 2, 3):
        src = (x + dx) % 4
        pltpu.make_async_remote_copy(
            src_ref=fin.at[x], dst_ref=fin.at[src], send_sem=s_f.at[0], recv_sem=r_f.at[src],
            device_id=device(dx=dx), device_id_type=MESH,
        ).wait_recv()
    for part in range(4):
        for half in (0, 1):
            at = (pl.ds(part * CHUNK, CHUNK), pl.ds(half * PAIR, PAIR))
            out_ref[at] = fin[part, half]

    for cp in started:
        cp.wait_send()
    for i, d in enumerate(DIST):
        over_y(i).wait_send()
        at = (z + d + 8) % 8

        @pl.when(at // 2 != x)
        def _():
            final(i, at % 2, at // 2).wait_send()


def body(sectors, environment, wavefunction):
    dma = pltpu.SemaphoreType.DMA
    pairs = []
    for link in ("zp", "zm", "y", "c"):
        pairs += [dma((len(LINKS[link]),)), dma((len(LINKS[link]),))]
    return pl.pallas_call(
        kernel,
        out_shape=jax.ShapeDtypeStruct((ROWS, TILE), jnp.bfloat16),
        in_specs=[
            pl.BlockSpec(memory_space=pltpu.SMEM),
            pl.BlockSpec(memory_space=pl.ANY),
            pl.BlockSpec(memory_space=pl.ANY),
        ],
        out_specs=pl.BlockSpec(memory_space=pltpu.VMEM),
        scratch_shapes=[
            pltpu.VMEM((ROWS, DEPTH), jnp.bfloat16),
            pltpu.VMEM((32 * ITEM, DEPTH), jnp.bfloat16),
            pltpu.VMEM((16, ROWS, PAIR), jnp.bfloat16),
            pltpu.VMEM((16, 4, CHUNK, PAIR), jnp.bfloat16),
            pltpu.VMEM((8, CHUNK, PAIR), jnp.float32),
            pltpu.VMEM((8, CHUNK, PAIR), jnp.bfloat16),
            pltpu.VMEM((8, CHUNK, PAIR), jnp.bfloat16),
            pltpu.VMEM((8, CHUNK, PAIR), jnp.bfloat16),
            pltpu.VMEM((4, 2, CHUNK, PAIR), jnp.bfloat16),
            *pairs,
            dma((16, 4)), dma((16, 4)), dma((8,)), dma((8,)), dma((8,)), dma((4,)), dma((2,)),
        ],
        compiler_params=pltpu.CompilerParams(
            collective_id=0, has_side_effects=True, vmem_limit_bytes=56 << 20
        ),
    )(sectors, environment, wavefunction.T)


def solution(mesh):
    placed = (P(), P("col", "row"), P("row", "col"))
    return jax.shard_map(
        body, mesh=mesh, in_specs=placed, out_specs=P("col", "row"), check_vma=False
    )
```

time: 216 us -> 87.2 us (0.40); the launches traced: 213 us -> 87 us
  waiting for transfers between devices: 156 us -> 0 us
  Pallas kernels: 0 us -> 85.3 us
  matrix products: 15.5 us -> 0 us
  blocking collectives: 13.4 us -> 0 us
  between operations: 13.4 us -> 0.01 us
  local copies, waits for them, and re-layouts: 9.97 us -> 1.77 us
  other arithmetic: 4.82 us -> 0 us
    pallas_call x0 -> x1, Pallas kernels: none -> 85.3 us  [body(): pl.pallas_call(kernel, out_shape=jax.ShapeDtypeStruct((ROWS, TILE), jnp.b...]
    reduce_scatter x1 -> x0, waiting for transfers between devices: 83.9 us -> none  [body(): lax.psum_scatter(jnp.dot(masked, gathered, preferred_element_type=jnp.flo...]
    all_gather x1 -> x0, waiting for transfers between devices: 71.4 us -> none  [body(): gathered = lax.all_gather(wavefunction, 'col', axis=1, tiled=True)]
    dot_general x1 -> x0, matrix products: 15.5 us -> none  [body(): jnp.dot(masked, gathered, preferred_element_type=jnp.float32)]
    all_to_all x1 -> x0, blocking collectives: 13.4 us -> none  [body(): lax.all_to_all(reduced, 'row', split_axis=1, concat_axis=0, tiled=True)]
    unnamed x5 -> x1, local copies, waits for them, and re-layouts: 7.49 us -> 1.77 us
    select_n x1 -> x0, other arithmetic: 4.75 us -> none  [body(): masked = jnp.where(allowed, environment, jnp.zeros_like(environment))]
  transfers between devices with their start and end apart: 2 -> 0, of which waited for: 2 -> 0; matrix products, arithmetic and copies ran while one was open for 6% -> 0% of each run, Pallas kernels for 0% -> 0%
where the time goes in v2:
time: 87.2 us; the launch traced here: 87 us
  Pallas kernels  85.3 us (98%)
  local copies, waits for them, and re-layouts  1.77 us (2%)
    pallas_call x1, Pallas kernels, body(): pl.pallas_call(kernel, out_shape=jax.ShapeDtypeStruct((ROWS, TILE), jnp.b...  85.3 us
    unnamed x1, local copies, waits for them, and re-layouts  1.77 us

profile of v2, /device:TPU:12, one launch (start us, length us, event | category | flops | bytes accessed | tf_op | source)
XLA Modules:
  0.0 87.0 jit_solution(1361583399178249807)
XLA Ops:
  0.0 85.3 %shard_map.37 = bf16[768,256]{1,0:T(8,128)(2,1)} custom-call(s32[96]{0:T(128)} %sec_ref.1, bf16[768,3072]{1,0:T(8,128)(2,1)} %env_ref.1, bf16[64,3072]{1,0:T(8,128)(2,1)} %bitcast.1), custom_call_target="tpu_custom_call" | custom-call | tf_op jit(solution)/shard_map/pallas_call | solution.py:296
  85.3 1.8 %copy.5 = bf16[768,256]{1,0:T(8,128)(2,1)} copy(bf16[768,256]{1,0:T(8,128)(2,1)} %shard_map.37) | data formatting | bytes 786432

commit v3 on v2

--- a/solution.py
+++ b/solution.py
@@ -14,6 +14,7 @@
 HALF = DEPTH // 2
 TILE = 256
 CHUNK = ROWS // 4
+STEP = 256
 
 H0 = (0, ITEM, 0, HALF)
 H1 = (0, ITEM, HALF, HALF)
@@ -44,55 +45,55 @@
     ("zp", 0, -2, H0),
     ("zm", 0, 2, H0),
     ("mm", 1, 0),
-    ("ra", 0, -1),
     ("zp", 1, -1, H1),
     ("zm", 1, 1, H1),
     ("y", 1, 1, H0),
+    ("ra", 0, -1),
+    ("mm", 1, -1),
     ("ra", 0, 1),
-    ("mm", 1, -1),
     ("mm", 1, 1),
     ("zp", 0, -2, H1),
     ("zm", 0, 2, H1),
     ("y", 1, -2, H0),
     ("ra", 1, 0),
     ("mm", 0, -2),
-    ("mm", 0, 2),
     ("zp", 0, -3, H0),
     ("zm", 0, 3, H0),
+    ("ra", 1, -1),
     ("y", 1, 2, H0),
-    ("ra", 1, -1),
+    ("mm", 0, 2),
     ("ra", 1, 1),
     ("rb", 0),
-    ("ra", 0, -2),
     ("zp", 1, -2, H1),
     ("zm", 1, 2, H1),
+    ("ra", 0, -2),
     ("mm", 1, -2),
     ("y", 1, -3, H0),
-    ("ra", 0, 2),
     ("mm", 1, 2),
     ("zp", 0, -3, H1),
     ("zm", 0, 3, H1),
+    ("ra", 0, 2),
+    ("y", 1, 3, H0),
     ("mm", 0, -3),
-    ("y", 1, 3, H0),
-    ("ra", 1, -2),
     ("rb", -1),
     ("zm", 1, 3, H1),
     ("zp", 0, 4, H0),
     ("rb", 1),
+    ("ra", 1, -2),
     ("mm", 0, 3),
     ("ra", 1, 2),
     ("mm", 1, 3),
-    ("rb", -2),
-    ("ra", 0, -3),
     ("zp", 1, -3, H1),
     ("zm", 0, 4, H1),
+    ("ra", 0, -3),
     ("mm", 1, -3),
+    ("zm", 1, 4, HI),
     ("y", 1, 4, H0),
-    ("zm", 1, 4, HI),
-    ("ra", 0, 3),
-    ("rb", 2),
     ("mm", 0, 4),
     ("zp", 1, 4, LO),
+    ("rb", -2),
+    ("rb", 2),
+    ("ra", 0, 3),
     ("ra", 1, 3),
     ("mm", 1, 4),
     ("ra", 1, -3),
@@ -178,13 +179,30 @@
             recv("c", line, d, part)
         t = DIST.index(d) * 2 + line
         base = (y + line) % 2 * (16 * ITEM) + (z + d + 8) % 8 * PAIR
-        block = g[pl.ds(pl.multiple_of(base, PAIR), PAIR), :]
-        cb[t] = lax.dot_general(
-            a[...], block, (((1,), (1,)), ((), ())), preferred_element_type=jnp.float32
-        ).astype(jnp.bfloat16)
+        block = pl.ds(pl.multiple_of(base, PAIR), PAIR)
+
+        step = CHUNK if d == 4 else STEP
+
+        def rows(m, _):
+            far = 2 - m + m // 2 * (3 - 2 * (m % 2))
+            at = (x + far) % 4 if d == 4 else m
+            at = pl.ds(pl.multiple_of(at * step, step), step)
+            cb[t, at, :] = lax.dot_general(
+                a[at, :], g[block, :], (((1,), (1,)), ((), ())), preferred_element_type=jnp.float32
+            ).astype(jnp.bfloat16)
+            if d == 4:
+
+                @pl.when(far != 0)
+                def _():
+                    share(t, far, (x + far) % 4, x).start()
+
+            return 0
+
+        lax.fori_loop(0, ROWS // step, rows, 0)
         for dx in (2, 1, 3):
             cp = share(t, dx, (x + dx) % 4, x)
-            cp.start()
+            if d != 4:
+                cp.start()
             started.append(cp)
 
     def share(t, dx, chunk, slot):
@@ -295,7 +313,7 @@
         pairs += [dma((len(LINKS[link]),)), dma((len(LINKS[link]),))]
     return pl.pallas_call(
         kernel,
-        out_shape=jax.ShapeDtypeStruct((ROWS, TILE), jnp.bfloat16),
+        out_shape=pltpu.VMEM((ROWS, TILE), jnp.bfloat16),
         in_specs=[
             pl.BlockSpec(memory_space=pltpu.SMEM),
             pl.BlockSpec(memory_space=pl.ANY),

time: 87.2 us -> 77.6 us (0.89)
  Pallas kernels: 85.3 us -> 76.7 us
  local copies, waits for them, and re-layouts: 1.77 us -> 0.75 us
    pallas_call x1, Pallas kernels: 85.3 us -> 76.7 us  [body(): pl.pallas_call(kernel, out_shape=pltpu.VMEM((ROWS, TILE), jnp.bfloat16),...]
    unnamed x1, local copies, waits for them, and re-layouts: 1.77 us -> 0.75 us
where the time goes in v3:
time: 77.6 us; the launch traced here: 77.5 us
  Pallas kernels  76.7 us (99%)
    pallas_call x1, Pallas kernels, body(): pl.pallas_call(kernel, out_shape=pltpu.VMEM((ROWS, TILE), jnp.bfloat16),...  76.7 us

profile of v3, /device:TPU:12, one launch (start us, length us, event | category | flops | bytes accessed | tf_op | source)
XLA Modules:
  0.0 77.5 jit_solution(14320548096345173450)
XLA Ops:
  0.0 76.7 %shard_map.37 = bf16[768,256]{1,0:T(8,128)(2,1)S(1)} custom-call(s32[96]{0:T(128)} %sec_ref.1, bf16[768,3072]{1,0:T(8,128)(2,1)} %env_ref.1, bf16[64,3072]{1,0:T(8,128)(2,1)} %bitcast.1), custom_call_target="tpu_custom_call" | custom-call | tf_op jit(solution)/shard_map/pallas_call | solution.py:314
  76.7 0.7 copy.5

commit v4 on v3

--- a/solution.py
+++ b/solution.py
@@ -11,15 +11,15 @@
 PAIR = 2 * ITEM
 ROWS = 768
 DEPTH = 3072
-HALF = DEPTH // 2
+HALF = 1664
 TILE = 256
 CHUNK = ROWS // 4
 STEP = 256
 
 H0 = (0, ITEM, 0, HALF)
-H1 = (0, ITEM, HALF, HALF)
-LO = (0, ITEM // 2, HALF, HALF)
-HI = (ITEM // 2, ITEM // 2, HALF, HALF)
+H1 = (0, ITEM, HALF, DEPTH - HALF)
+LO = (0, ITEM // 2, HALF, DEPTH - HALF)
+HI = (ITEM // 2, ITEM // 2, HALF, DEPTH - HALF)
 
 DIST = [0, -1, 1, -2, 2, -3, 3, 4]
 
@@ -32,75 +32,75 @@
 
 ORDER = [
     ("mm", 0, 0),
+    ("y", 1, 0, H1),
     ("zp", 0, -1, H0),
     ("zm", 0, 1, H0),
-    ("y", 1, 0, H1),
     ("ra", 0, 0),
     ("zp", 0, -1, H1),
     ("zm", 0, 1, H1),
     ("y", 1, 0, H0),
     ("mm", 0, -1),
+    ("zp", 1, -1, H1),
+    ("zm", 1, 1, H1),
     ("mm", 0, 1),
     ("y", 1, -1, H0),
+    ("mm", 1, 0),
+    ("mm", 1, -1),
+    ("y", 1, 1, H0),
     ("zp", 0, -2, H0),
     ("zm", 0, 2, H0),
-    ("mm", 1, 0),
-    ("zp", 1, -1, H1),
-    ("zm", 1, 1, H1),
-    ("y", 1, 1, H0),
     ("ra", 0, -1),
-    ("mm", 1, -1),
-    ("ra", 0, 1),
     ("mm", 1, 1),
+    ("ra", 1, 0),
     ("zp", 0, -2, H1),
     ("zm", 0, 2, H1),
+    ("ra", 0, 1),
+    ("mm", 0, -2),
     ("y", 1, -2, H0),
-    ("ra", 1, 0),
-    ("mm", 0, -2),
+    ("zm", 1, 2, H1),
+    ("mm", 0, 2),
+    ("ra", 1, -1),
+    ("ra", 1, 1),
+    ("y", 1, 2, H0),
+    ("zm", 0, 3, H0),
     ("zp", 0, -3, H0),
-    ("zm", 0, 3, H0),
-    ("ra", 1, -1),
-    ("y", 1, 2, H0),
-    ("mm", 0, 2),
-    ("ra", 1, 1),
-    ("rb", 0),
     ("zp", 1, -2, H1),
-    ("zm", 1, 2, H1),
-    ("ra", 0, -2),
-    ("mm", 1, -2),
-    ("y", 1, -3, H0),
     ("mm", 1, 2),
     ("zp", 0, -3, H1),
     ("zm", 0, 3, H1),
+    ("mm", 1, -2),
+    ("mm", 0, -3),
+    ("y", 1, 3, H0),
+    ("zm", 1, 3, H1),
+    ("mm", 0, 3),
+    ("zp", 0, 4, H0),
+    ("mm", 1, 3),
+    ("zm", 0, 4, H1),
+    ("y", 1, -3, H0),
+    ("zp", 1, -3, H1),
+    ("mm", 0, 4),
+    ("zm", 1, 4, HI),
+    ("mm", 1, -3),
+    ("y", 1, 4, H0),
+    ("zp", 1, 4, LO),
+    ("ra", 0, -2),
+    ("ra", 1, 2),
+    ("ra", 1, -2),
+    ("ra", 0, -3),
+    ("mm", 1, 4),
+    ("ra", 0, 3),
+    ("ra", 0, 4),
+    ("rb", -1),
+    ("rb", 1),
+    ("rb", -2),
+    ("ra", 1, -3),
+    ("ra", 1, 3),
     ("ra", 0, 2),
-    ("y", 1, 3, H0),
-    ("mm", 0, -3),
-    ("rb", -1),
-    ("zm", 1, 3, H1),
-    ("zp", 0, 4, H0),
-    ("rb", 1),
-    ("ra", 1, -2),
-    ("mm", 0, 3),
-    ("ra", 1, 2),
-    ("mm", 1, 3),
-    ("zp", 1, -3, H1),
-    ("zm", 0, 4, H1),
-    ("ra", 0, -3),
-    ("mm", 1, -3),
-    ("zm", 1, 4, HI),
-    ("y", 1, 4, H0),
-    ("mm", 0, 4),
-    ("zp", 1, 4, LO),
-    ("rb", -2),
+    ("rb", 0),
+    ("ra", 1, 4),
+    ("rb", -3),
+    ("rb", 3),
     ("rb", 2),
-    ("ra", 0, 3),
-    ("ra", 1, 3),
-    ("mm", 1, 4),
-    ("ra", 1, -3),
-    ("rb", 3),
-    ("ra", 0, 4),
-    ("rb", -3),
-    ("ra", 1, 4),
     ("rb", 4),
 ]
 

time: 77.6 us -> 74.3 us (0.957)
  Pallas kernels: 76.7 us -> 73.2 us
    pallas_call x1, Pallas kernels: 76.7 us -> 73.2 us  [body(): pl.pallas_call(kernel, out_shape=pltpu.VMEM((ROWS, TILE), jnp.bfloat16),...]
where the time goes in v4:
time: 74.3 us; the launch traced here: 73.9 us
  Pallas kernels  73.2 us (99%)
  local copies, waits for them, and re-layouts  0.75 us (1%)
    pallas_call x1, Pallas kernels, body(): pl.pallas_call(kernel, out_shape=pltpu.VMEM((ROWS, TILE), jnp.bfloat16),...  73.2 us

profile of v4, /device:TPU:12, one launch (start us, length us, event | category | flops | bytes accessed | tf_op | source)
XLA Modules:
  0.0 73.9 jit_solution(3842110594151809432)
XLA Ops:
  0.0 73.2 %shard_map.37 = bf16[768,256]{1,0:T(8,128)(2,1)S(1)} custom-call(s32[96]{0:T(128)} %sec_ref.1, bf16[768,3072]{1,0:T(8,128)(2,1)} %env_ref.1, bf16[64,3072]{1,0:T(8,128)(2,1)} %bitcast.1), custom_call_target="tpu_custom_call" | custom-call | tf_op jit(solution)/shard_map/pallas_call | solution.py:314
  73.2 0.7 %copy.5 = bf16[768,256]{1,0:T(8,128)(2,1)} copy(bf16[768,256]{1,0:T(8,128)(2,1)S(1)} %shard_map.37) | data formatting | bytes 786432

commit v5 on v4

--- a/solution.py
+++ b/solution.py
@@ -84,19 +84,19 @@
     ("y", 1, 4, H0),
     ("zp", 1, 4, LO),
     ("ra", 0, -2),
+    ("ra", 0, 2),
     ("ra", 1, 2),
     ("ra", 1, -2),
     ("ra", 0, -3),
     ("mm", 1, 4),
     ("ra", 0, 3),
     ("ra", 0, 4),
+    ("rb", 0),
     ("rb", -1),
     ("rb", 1),
     ("rb", -2),
     ("ra", 1, -3),
     ("ra", 1, 3),
-    ("ra", 0, 2),
-    ("rb", 0),
     ("ra", 1, 4),
     ("rb", -3),
     ("rb", 3),

time: 74.3 us -> 74.3 us (level)
  no operation moved by 1% of the time
where the time goes in v5:
time: 74.3 us; the launch traced here: 73.8 us
  Pallas kernels  73.1 us (98%)
  local copies, waits for them, and re-layouts  0.75 us (1%)
    pallas_call x1, Pallas kernels, body(): pl.pallas_call(kernel, out_shape=pltpu.VMEM((ROWS, TILE), jnp.bfloat16),...  73.1 us

profile of v5, /device:TPU:12, one launch (start us, length us, event | category | flops | bytes accessed | tf_op | source)
XLA Modules:
  0.0 73.8 jit_solution(1883622165797567025)
XLA Ops:
  0.0 73.1 %shard_map.37 = bf16[768,256]{1,0:T(8,128)(2,1)S(1)} custom-call(s32[96]{0:T(128)} %sec_ref.1, bf16[768,3072]{1,0:T(8,128)(2,1)} %env_ref.1, bf16[64,3072]{1,0:T(8,128)(2,1)} %bitcast.1), custom_call_target="tpu_custom_call" | custom-call | tf_op jit(solution)/shard_map/pallas_call | solution.py:314
  73.1 0.7 %copy.5 = bf16[768,256]{1,0:T(8,128)(2,1)} copy(bf16[768,256]{1,0:T(8,128)(2,1)S(1)} %shard_map.37) | data formatting | bytes 786432
